TPU v7x, 512 devices: a whole 4x4x16 slice. The times are simulated.
512 devices in a mesh: fsdp: 8 (over y, x_lo), tensor: 64 (over x_hi, z, core).
Axes of the slice: x: 4 (x_hi: 2, x_lo: 2; x = x_hi * 2 + x_lo), y: 4, z: 16, core: 2. Of those that a mesh axis runs over, the one named last changes fastest.
Arguments:
- tokens: bfloat16 [1024, 8192], P('fsdp', 'tensor'), may hold values from -6 to 6
- in_values: bfloat16 [8192, 3, 8192], P('fsdp', None, 'tensor'), may hold values from -0.1875 to 0.1875
- in_scales: bfloat16 [64, 3, 8192], P('fsdp', None, 'tensor'), may hold values from 0.5 to 2
- filters: float32 [512, 128], P('tensor'), may hold values from -0.6 to 0.6
- out_weight: bfloat16 [8192, 8192], P('tensor', 'fsdp'), may hold values from -0.0625 to 0.0625
- cotangent: bfloat16 [1024, 8192], P('fsdp', 'tensor'), may hold values from -15 to 15
Outputs:
- input_grad: bfloat16 [1024, 8192], P('fsdp', 'tensor')
- filter_grad: float32 [512, 128], P('tensor')
All inputs are finite; a program needn't handle non-finite values.
Results may differ from a plain program's by a relative error of at most 0.012.
Values may be sent and summed in bfloat16 or wider, within the bound.
A program may use at most 128 MiB of HBM per device.

v0:
```python
import jax
import jax.numpy as jnp
from jax import lax
from jax.sharding import PartitionSpec as P

BLOCK = 128


def passed_along(array, axis, by):
    length = lax.axis_size(axis)
    pairs = [(i, i + by) for i in range(length) if 0 <= i + by < length]
    return lax.ppermute(array, axis, pairs)


def dequantize(values, scales):
    blocks = scales.shape[0]
    channels = values.shape[2]
    scaled = (
        values.astype(jnp.float32).reshape(blocks, BLOCK, 3, channels)
        * scales.astype(jnp.float32)[:, None]
    )
    return scaled.reshape(blocks * BLOCK, 3 * channels).astype(jnp.bfloat16)


def apply_taps(filt, extended, rows, per_group, causal):
    taps = filt.shape[1]
    repeated = jnp.repeat(filt, per_group, axis=0)

    def one_step(lag_index, total):
        lag_value = jnp.asarray(lag_index).astype(jnp.int32)
        offset = taps - 1 - lag_value if causal else lag_value
        slab = lax.dynamic_slice_in_dim(extended, offset, rows, 0)
        column = lax.dynamic_slice_in_dim(repeated, lag_value, 1, 1)[:, 0]
        return total + column[None, :] * slab

    return lax.fori_loop(0, taps, one_step, jnp.zeros((rows, repeated.shape[0]), jnp.float32))


def filter_terms(grad_rows, extended, groups_here, per_group, taps):
    rows = grad_rows.shape[0]
    ext_rows = extended.shape[0]
    corr = jnp.einsum(
        "tgj,ugj->gtu",
        grad_rows.reshape(rows, groups_here, per_group),
        extended.reshape(ext_rows, groups_here, per_group),
        precision=lax.Precision.HIGHEST,
    )
    flat = jnp.concatenate(
        [corr.reshape(groups_here, rows * ext_rows), jnp.zeros((groups_here, rows), jnp.float32)], 1
    )
    diagonal = flat.reshape(groups_here, rows, ext_rows + 1)[:, :, :taps]
    return jnp.sum(diagonal, axis=1)[:, ::-1]


def fetch_out(out_weight):
    return lax.all_gather(out_weight, "fsdp", axis=1, tiled=True)


def on_device(tokens, in_values, in_scales, filters, out_weight, cotangent):
    rows = tokens.shape[0]
    channels = tokens.shape[1]
    groups_here, taps = filters.shape
    per_group = channels // groups_here
    whole = lax.all_gather(tokens, "tensor", axis=1, tiled=True)
    values, scales = (
        lax.all_gather(in_values, "fsdp", axis=0, tiled=True),
        lax.all_gather(in_scales, "fsdp", axis=0, tiled=True),
    )
    weight = dequantize(values, scales)
    proj = (
        jnp.dot(whole, weight, preferred_element_type=jnp.float32)
        .astype(jnp.bfloat16)
        .reshape(rows, 3, channels)
    )
    query = proj[:, 0].astype(jnp.float32)
    key_part = proj[:, 1].astype(jnp.float32)
    value_part = proj[:, 2].astype(jnp.float32)
    product = key_part * value_part
    earlier = passed_along(product[rows - (taps - 1) :].astype(jnp.bfloat16), "fsdp", 1).astype(
        jnp.float32
    )
    extended = jnp.concatenate([earlier, product], 0)
    conv = apply_taps(filters, extended, rows, per_group, True)
    out_full = fetch_out(out_weight)
    cot_whole = lax.all_gather(cotangent, "tensor", axis=1, tiled=True)
    grad_z = lax.dot_general(
        cot_whole, out_full, (((1,), (1,)), ((), ())), preferred_element_type=jnp.float32
    )
    grad_query = grad_z * conv
    grad_conv = grad_z * query
    following = passed_along(grad_conv[: taps - 1].astype(jnp.bfloat16), "fsdp", -1).astype(
        jnp.float32
    )
    grad_ext = jnp.concatenate([grad_conv, following], 0)
    grad_product = apply_taps(filters, grad_ext, rows, per_group, False)
    grad_proj = jnp.stack([grad_query, grad_product * value_part, grad_product * key_part], axis=1)
    grad_proj = grad_proj.astype(jnp.bfloat16).reshape(rows, 3 * channels)
    summed = lax.psum_scatter(
        lax.dot_general(
            weight, grad_proj, (((1,), (1,)), ((), ())), preferred_element_type=jnp.float32
        ),
        "tensor",
        scatter_dimension=0,
        tiled=True,
    )
    input_grad = summed.T.astype(jnp.bfloat16)
    local_filter = filter_terms(grad_conv, extended, groups_here, per_group, taps) / rows
    filter_grad = lax.psum(local_filter, "fsdp")
    return (input_grad, filter_grad)


def solution(mesh):
    placed = (
        P("fsdp", "tensor"),
        P("fsdp", None, "tensor"),
        P("fsdp", None, "tensor"),
        P("tensor", None),
        P("tensor", "fsdp"),
        P("fsdp", "tensor"),
    )
    return jax.shard_map(
        on_device,
        mesh=mesh,
        in_specs=placed,
        out_specs=(P("fsdp", "tensor"), P("tensor", None)),
        check_vma=False,
    )
```

profile of v0, /device:TPU:8, one launch (start us, length us, event | category | flops | bytes accessed | tf_op | source)
XLA Modules:
  0.0 812.5 jit_solution(18194216193005715439)
XLA Ops:
  7.2 2.3 copy.16
  9.6 0.7 all-gather.11.cloned.1.call-update
  10.3 0.7 all-gather.9.cloned.1.call-update
  11.1 0.5 all-gather.7.cloned.1.call-update
  11.7 29.2 %all_gather.16 = bf16[64,3,128]{2,0,1:T(8,128)(2,1)S(1)} all-gather(bf16[8,3,128]{2,0,1:T(8,128)(2,1)} %param.12), channel_id=1, replica_groups=mesh['fsdp'=8,'tensor'=64] {'fsdp'}, dimensions={0}, use_global_device_ids=true | all-gather | bytes 55296 | tf_op jit(solution)/shard_map/all_gather | solution.py:67
  40.8 0.1 copy.17
  41.0 110.4 %all-gather.5.cloned.1.call-done = bf16[8192,3,128]{0,2,1:T(8,128)(2,1)} async-done(((bf16[1024,3,128]{0,2,1:T(8,128)(2,1)}), bf16[8192,3,128]{0,2,1:T(8,128)(2,1)}) %all-gather.5.cloned.1.call-update) | async-done | bytes 6291472 | tf_op jit(solution)/shard_map/all_gather | solution.py:66
  151.4 7.2 mul.88
  158.6 16.8 %fusion = bf16[8192,384]{0,1:T(8,128)(2,1)} fusion(f32[48,8,64,128]{3,2,1,0:T(8,128)} %bitcast.64, bf16[8192,3,128]{0,2,1:T(8,128)(2,1)} %all-gather.5.cloned.1.call-done), kind=kLoop, calls=%fused_computation.7 | loop fusion | flops 9437184 | bytes 25165824 | tf_op jit(solution)/shard_map/convert_element_type | solution.py:22
  175.3 117.4 %all-gather.11.cloned.1.call-done = bf16[128,8192]{1,0:T(8,128)(2,1)} async-done(((bf16[128,128]{1,0:T(8,128)(2,1)}), bf16[128,8192]{1,0:T(8,128)(2,1)}) %all-gather.11.cloned.1.call-update) | async-done | bytes 2097168 | tf_op jit(solution)/shard_map/all_gather | solution.py:64
  292.7 5.2 convolution_convert_fusion
  297.9 49.0 %all-gather.9.cloned.1.call-done = bf16[128,8192]{1,0:T(8,128)(2,1)} async-done(((bf16[128,1024]{1,0:T(8,128)(2,1)}), bf16[128,8192]{1,0:T(8,128)(2,1)}) %all-gather.9.cloned.1.call-update) | async-done | bytes 2097168 | tf_op jit(solution)/shard_map/all_gather | solution.py:56
  347.0 141.2 %all-gather.7.cloned.1.call-done = bf16[128,8192]{1,0:T(8,128)(2,1)} async-done(((bf16[128,128]{1,0:T(8,128)(2,1)}), bf16[128,8192]{1,0:T(8,128)(2,1)}) %all-gather.7.cloned.1.call-update) | async-done | bytes 2097168 | tf_op jit(solution)/shard_map/all_gather | solution.py:85
  488.2 2.9 convert_multiply_fusion.1
  491.2 2.7 collective-permute-start
  493.9 13.8 %mul.89 = f32[8192,3,128]{0,2,1:T(8,128)} reshape(f32[64,128,3,128]{1,0,3,2:T(8,128)} %mul.88) | data formatting | bytes 25165824 | tf_op jit(solution)/shard_map/mul | solution.py:19
  507.8 4.3 collective-permute-start.1
  512.1 0.1 pad_maximum_fusion
  512.2 33.2 %while.30 = (s32[]{:T(128)}, f32[128,128]{1,0:T(8,128)S(1)}, f32[128,128]{0,1:T(8,128)S(1)}, f32[255,128]{0,1:T(8,128)S(1)}, s32[]{:T(128)}, /*index=5*/s32[]{:T(128)}, s32[]{:T(128)}, s32[]{:T(128)}) while((s32[]{:T(128)}, f32[128,128]{1,0:T(8,128)S(1)}, f32[128,128]{0,1:T(8,128)S(1)}, f32[255,128]{0,1:T(8,128)S(1)}, s32[]{:T(128)}, ...), condition=%wide.region_1.0_spmd.clone, body=%wide.region_0.0_spmd.clone.sunk | while | flops 49159 | bytes 460437 | solution.py:36
  512.3 0.1 copy.36
  513.1 0.1 copy.36
  513.9 0.1 copy.36
  514.7 0.1 copy.36
  515.5 0.1 copy.36
  516.2 0.1 copy.36
  517.0 0.1 copy.36
  517.3 0.1 copy.36
  518.1 0.1 copy.36
  518.8 0.1 copy.36
  519.6 0.1 copy.36
  520.4 0.1 copy.36
  521.2 0.1 copy.36
  522.0 0.1 copy.36
  522.2 0.1 copy.36
  523.0 0.1 copy.36
  523.8 0.1 copy.36
  524.5 0.1 copy.36
  525.3 0.1 copy.36
  526.1 0.1 copy.36
  545.6 32.5 %while.31 = (s32[]{:T(128)}, f32[128,128]{1,0:T(8,128)S(1)}, f32[128,128]{0,1:T(8,128)S(1)}, f32[255,128]{0,1:T(8,128)S(1)}, s32[]{:T(128)}, /*index=5*/s32[]{:T(128)}) while((s32[]{:T(128)}, f32[128,128]{1,0:T(8,128)S(1)}, f32[128,128]{0,1:T(8,128)S(1)}, f32[255,128]{0,1:T(8,128)S(1)}, s32[]{:T(128)}, /*index=5*/s32[]{:T(128)}) %tuple.96), condition=%wide.region_3.0_spmd.clone, body=%wide.region_2.0_spmd.clone.sunk | while | flops 49155 | bytes 460375 | solution.py:36
  578.3 10.5 %convolution_bitcast_fusion = f32[8192,128]{1,0:T(8,128)} fusion(f32[8192,3,128]{0,2,1:T(8,128)} %mul.89, bf16[8192,3,128]{0,2,1:T(8,128)(2,1)} %all-gather.5.cloned.1.call-done, bf16[128,1,128]{0,2,1:T(8,128)(2,1)S(1)} %get-tuple-element.260, bf16[128,1,128]{0,2,1:T(8,128)(2,1)S(1)} %get-tuple-element.259, bf16[128,1,128]{0,2,1:T(8,128)(2,1)S(1)} %fusion.9), kind=kOutput, calls=%fused_computation.9 | convolution fusion | flops 814841856 | bytes 23166976 | tf_op jit(solution)/shard_map/dot_general | solution.py:99
  588.8 1.0 fusion.13
  589.8 0.6 reshape.48
  590.5 0.1 slice_reduce_fusion
  590.7 16.3 %psum.7 = f32[8,128]{1,0:T(8,128)} all-reduce(f32[8,128]{1,0:T(8,128)S(1)} %broadcast_multiply_fusion), channel_id=1, replica_groups=mesh['fsdp'=8,'tensor'=64] {'fsdp'}, use_global_device_ids=true, to_apply=%region_6.0 | all-reduce | flops 1024 | bytes 8192 | tf_op jit(solution)/shard_map/psum | solution.py:108
  607.0 197.4 %reduce-scatter.2.cloned.1.call-done = f32[128,128]{1,0:T(8,128)} async-done(((f32[8192,128]{1,0:T(8,128)}), f32[128,128]{1,0:T(8,128)}) %reduce-scatter.2.cloned.1.call-update) | async-done | bytes 65552 | tf_op jit(solution)/shard_map/reduce_scatter | solution.py:98
  804.4 0.8 convert_bitcast_fusion
  805.2 0.7 copy.27
  (1031 shorter events, 52.0 us)
Async XLA Ops:
  7.2 144.2 %all-gather.5.cloned.1.call-start = ((), (), s32[]{:S(2)}) async-start(), calls=%async_computation.1 | async-start | bytes 7077888 | tf_op jit(solution)/shard_map/all_gather | solution.py:66
  9.5 283.2 %all-gather.11.cloned.1.call-start = ((), (), s32[]{:S(2)}) async-start(), calls=%async_computation.4 | async-start | bytes 2129920 | tf_op jit(solution)/shard_map/all_gather | solution.py:64
  10.3 336.7 %all-gather.9.cloned.1.call-start = ((), (), s32[]{:S(2)}) async-start(), calls=%async_computation.3 | async-start | bytes 2359296 | tf_op jit(solution)/shard_map/all_gather | solution.py:56
  11.0 477.2 %all-gather.7.cloned.1.call-start = ((), (), s32[]{:S(2)}) async-start(), calls=%async_computation.2 | async-start | bytes 2129920 | tf_op jit(solution)/shard_map/all_gather | solution.py:85
  11.6 792.8 %reduce-scatter.2.cloned.1.call-start = ((), (), s32[]{:S(2)}) async-start(), calls=%async_computation.5 | async-start | bytes 4259840 | tf_op jit(solution)/shard_map/reduce_scatter | solution.py:98
  491.2 20.9 %collective-permute-start = (bf16[127,128]{0,1:T(8,128)(2,1)S(1)}, bf16[127,128]{0,1:T(8,128)(2,1)S(1)}, u32[]{:S(2)}, u32[]{:S(2)}) collective-permute-start(bf16[127,128]{0,1:T(8,128)(2,1)S(1)} %slice.49), channel_id=1, source_target_pairs={{0,64},{64,128},{128,192},{192,256},{256,320},{320,384},{384,448},... | collective-permute-start | bytes 97544 | tf_op jit(solution)/shard_map/ppermute | solution.py:12
  493.9 13.8 %copy-start = (f32[8,128]{1,0:T(8,128)S(1)}, f32[8,128]{1,0:T(8,128)}, u32[]{:S(2)}) copy-start(f32[8,128]{1,0:T(8,128)} %param.13) | copy-start | bytes 12292
  507.8 37.7 %collective-permute-start.1 = (bf16[127,128]{0,1:T(8,128)(2,1)S(1)}, bf16[127,128]{0,1:T(8,128)(2,1)S(1)}, u32[]{:S(2)}, u32[]{:S(2)}) collective-permute-start(bf16[127,128]{0,1:T(8,128)(2,1)S(1)} %slice.48), channel_id=1, source_target_pairs={{64,0},{128,64},{192,128},{256,192},{320,256},{384,320},{448,384},... | collective-permute-start | bytes 97544 | tf_op jit(solution)/shard_map/ppermute | solution.py:12
Sparse Core Ops, SparseCore 0:
  10.1 141.2 all-gather.4
  154.4 138.2 all-gather.10
  294.8 52.1 all-gather.8
  349.8 138.3 all-gather.6
  588.9 215.4 reduce-scatter.1
where the time goes:
time: 813 us; the launch traced here: 812 us
  waiting for transfers between devices  617 us (76%)
  local copies, waits for them, and re-layouts  73.6 us (9%)
  blocking collectives  45.5 us (6%)
  other arithmetic  22.5 us (3%)
  matrix products  19.7 us (2%)
  between operations  14 us (2%)
  loops' own time  12.7 us (2%)
    reduce_scatter x1, waiting for transfers between devices, on_device(): lax.psum_scatter(lax.dot_general(weight, grad_proj, (((1,), (1,)), ((), (...  197 us
    all_gather x1, waiting for transfers between devices, on_device(): cot_whole = lax.all_gather(cotangent, 'tensor', axis=1, tiled=True)  141 us
    all_gather x1, waiting for transfers between devices, on_device(): whole = lax.all_gather(tokens, 'tensor', axis=1, tiled=True)  117 us
    all_gather x1, waiting for transfers between devices, on_device(): lax.all_gather(in_values, 'fsdp', axis=0, tiled=True)  110 us
    all_gather x1, waiting for transfers between devices, fetch_out(): return lax.all_gather(out_weight, 'fsdp', axis=1, tiled=True)  49 us
    dynamic_slice x512, local copies, waits for them, and re-layouts, one_step(): slab = lax.dynamic_slice_in_dim(extended, offset, rows, 0)  45.3 us
    all_gather x1, blocking collectives, on_device(): lax.all_gather(in_scales, 'fsdp', axis=0, tiled=True)  29.2 us
    mul x2, local copies, waits for them, and re-layouts, dequantize(): values.astype(jnp.float32).reshape(blocks, BLOCK, 3, channels)  21 us
  transfers between devices with their start and end apart: 7, of which 5 were waited for; matrix products, arithmetic and copies ran while one was open for 9% of the time, Pallas kernels for 0%

commit v1 on v0

--- a/solution.py
+++ b/solution.py
@@ -82,7 +82,10 @@
     extended = jnp.concatenate([earlier, product], 0)
     conv = apply_taps(filters, extended, rows, per_group, True)
     out_full = fetch_out(out_weight)
-    cot_whole = lax.all_gather(cotangent, "tensor", axis=1, tiled=True)
+    count = lax.axis_size("tensor")
+    pieces = jnp.stack([cotangent for _ in range(count)])
+    pieces = lax.all_to_all(pieces, "tensor", split_axis=0, concat_axis=0)
+    cot_whole = jnp.concatenate(pieces, axis=1)
     grad_z = lax.dot_general(
         cot_whole, out_full, (((1,), (1,)), ((), ())), preferred_element_type=jnp.float32
     )

time: 813 us -> 702 us (0.86)
  waiting for transfers between devices: 617 us -> 490 us
  starting transfers between devices: 7.11 us -> 25.6 us
    all_gather x1 -> x0, waiting for transfers between devices: 141 us -> none  [on_device(): cot_whole = lax.all_gather(cotangent, 'tensor', axis=1, tiled=True)]
    all_to_all x0 -> x1, starting transfers between devices: none -> 18.6 us  [on_device(): pieces = lax.all_to_all(pieces, 'tensor', split_axis=0, concat_axis=0)]
  transfers between devices with their start and end apart: 7 -> 7, of which waited for: 5 -> 4; matrix products, arithmetic and copies ran while one was open for 9% -> 11% of each run, Pallas kernels for 0% -> 0%
where the time goes in v1:
time: 702 us; the launch traced here: 701 us
  waiting for transfers between devices  490 us (70%)
  local copies, waits for them, and re-layouts  76.3 us (11%)
  blocking collectives  40.9 us (6%)
  starting transfers between devices  25.6 us (4%)
  other arithmetic  22.5 us (3%)
  matrix products  19 us (3%)
  between operations  14 us (2%)
  loops' own time  12.7 us (2%)
    reduce_scatter x1, waiting for transfers between devices, on_device(): lax.psum_scatter(lax.dot_general(weight, grad_proj, (((1,), (1,)), ((), (...  205 us
    all_gather x1, waiting for transfers between devices, on_device(): whole = lax.all_gather(tokens, 'tensor', axis=1, tiled=True)  118 us
    all_gather x1, waiting for transfers between devices, on_device(): lax.all_gather(in_values, 'fsdp', axis=0, tiled=True)  117 us
    all_gather x1, waiting for transfers between devices, fetch_out(): return lax.all_gather(out_weight, 'fsdp', axis=1, tiled=True)  49 us
    dynamic_slice x512, local copies, waits for them, and re-layouts, one_step(): slab = lax.dynamic_slice_in_dim(extended, offset, rows, 0)  45.3 us
    all_gather x1, blocking collectives, on_device(): lax.all_gather(in_scales, 'fsdp', axis=0, tiled=True)  24.6 us
    mul x2, local copies, waits for them, and re-layouts, dequantize(): values.astype(jnp.float32).reshape(blocks, BLOCK, 3, channels)  21 us
    all_to_all x1, starting transfers between devices, on_device(): pieces = lax.all_to_all(pieces, 'tensor', split_axis=0, concat_axis=0)  18.6 us
  transfers between devices with their start and end apart: 7, of which 4 were waited for; matrix products, arithmetic and copies ran while one was open for 11% of the time, Pallas kernels for 0%

profile of v1, /device:TPU:8, one launch (start us, length us, event | category | flops | bytes accessed | tf_op | source)
XLA Modules:
  0.0 701.5 jit_solution(14273591543560967045)
XLA Ops:
  7.2 2.3 copy.16
  9.6 0.9 copy.18
  10.4 1.8 stack.14
  12.2 18.6 %all-to-all-start = ((bf16[64,128,128]{1,2,0:T(8,128)(2,1)}), bf16[64,128,128]{1,2,0:T(8,128)(2,1)S(1)}, u32[]{:S(2)}, u32[]{:S(2)}) async-start(bf16[64,128,128]{1,2,0:T(8,128)(2,1)} %stack.14), calls=%async_computation | async-start | bytes 4194304 | tf_op jit(solution)/shard_map/all_to_all | solution.py:87
  30.9 0.7 all-gather.8.cloned.1.call-update
  31.6 0.7 all-gather.6.cloned.1.call-update
  32.4 24.6 %all_gather.13 = bf16[64,3,128]{2,0,1:T(8,128)(2,1)S(1)} all-gather(bf16[8,3,128]{2,0,1:T(8,128)(2,1)S(1)} %copy-done), channel_id=1, replica_groups=mesh['fsdp'=8,'tensor'=64] {'fsdp'}, dimensions={0}, use_global_device_ids=true | all-gather | bytes 55296 | tf_op jit(solution)/shard_map/all_gather | solution.py:67
  56.9 0.1 copy.17
  57.0 117.4 %all-gather.4.cloned.1.call-done = bf16[8192,3,128]{0,2,1:T(8,128)(2,1)} async-done(((bf16[1024,3,128]{0,2,1:T(8,128)(2,1)}), bf16[8192,3,128]{0,2,1:T(8,128)(2,1)}) %all-gather.4.cloned.1.call-update) | async-done | bytes 6291472 | tf_op jit(solution)/shard_map/all_gather | solution.py:66
  174.4 7.2 %mul.88 = f32[64,128,3,128]{1,0,3,2:T(8,128)} broadcast(f32[64,3,128]{0,2,1:T(8,128)S(1)} %copy.17), dimensions={0,2,3} | broadcast | bytes 12681216 | tf_op jit(solution)/shard_map/mul | solution.py:19
  181.6 16.8 %fusion = bf16[8192,384]{0,1:T(8,128)(2,1)} fusion(f32[48,8,64,128]{3,2,1,0:T(8,128)} %bitcast.67, bf16[8192,3,128]{0,2,1:T(8,128)(2,1)} %all-gather.4.cloned.1.call-done), kind=kLoop, calls=%fused_computation.7 | loop fusion | flops 9437184 | bytes 25165824 | tf_op jit(solution)/shard_map/convert_element_type | solution.py:22
  198.4 117.6 %all-gather.8.cloned.1.call-done = bf16[128,8192]{1,0:T(8,128)(2,1)} async-done(((bf16[128,128]{1,0:T(8,128)(2,1)}), bf16[128,8192]{1,0:T(8,128)(2,1)}) %all-gather.8.cloned.1.call-update) | async-done | bytes 2097168 | tf_op jit(solution)/shard_map/all_gather | solution.py:64
  316.0 5.2 convolution_convert_fusion
  321.2 49.0 %all-gather.6.cloned.1.call-done = bf16[128,8192]{1,0:T(8,128)(2,1)} async-done(((bf16[128,1024]{1,0:T(8,128)(2,1)}), bf16[128,8192]{1,0:T(8,128)(2,1)}) %all-gather.6.cloned.1.call-update) | async-done | bytes 2097168 | tf_op jit(solution)/shard_map/all_gather | solution.py:56
  370.2 2.3 convert_multiply_fusion.1
  372.6 3.4 collective-permute-start
  376.0 13.8 %mul.89 = f32[8192,3,128]{0,2,1:T(8,128)} reshape(f32[64,128,3,128]{1,0,3,2:T(8,128)} %mul.88) | data formatting | bytes 25165824 | tf_op jit(solution)/shard_map/mul | solution.py:19
  390.0 3.5 collective-permute-start.1
  393.5 0.1 pad_maximum_fusion
  393.6 33.2 %while.30 = (s32[]{:T(128)}, f32[128,128]{1,0:T(8,128)S(1)}, f32[128,128]{0,1:T(8,128)S(1)}, f32[255,128]{0,1:T(8,128)S(1)}, s32[]{:T(128)}, /*index=5*/s32[]{:T(128)}, s32[]{:T(128)}, s32[]{:T(128)}) while((s32[]{:T(128)}, f32[128,128]{1,0:T(8,128)S(1)}, f32[128,128]{0,1:T(8,128)S(1)}, f32[255,128]{0,1:T(8,128)S(1)}, s32[]{:T(128)}, ...), condition=%wide.region_1.0_spmd.clone, body=%wide.region_0.0_spmd.clone.sunk | while | flops 49159 | bytes 460437 | solution.py:36
  393.7 0.1 copy.37
  394.5 0.1 copy.37
  395.3 0.1 copy.37
  396.1 0.1 copy.37
  396.3 0.1 copy.37
  397.1 0.1 copy.37
  397.9 0.1 copy.37
  398.7 0.1 copy.37
  399.5 0.1 copy.37
  400.2 0.1 copy.37
  401.0 0.1 copy.37
  401.3 0.1 copy.37
  402.0 0.1 copy.37
  402.8 0.1 copy.37
  403.6 0.1 copy.37
  404.4 0.1 copy.37
  405.2 0.1 copy.37
  405.9 0.1 copy.37
  406.2 0.1 copy.37
  427.0 32.5 %while.31 = (s32[]{:T(128)}, f32[128,128]{1,0:T(8,128)S(1)}, f32[128,128]{0,1:T(8,128)S(1)}, f32[255,128]{0,1:T(8,128)S(1)}, s32[]{:T(128)}, /*index=5*/s32[]{:T(128)}) while((s32[]{:T(128)}, f32[128,128]{1,0:T(8,128)S(1)}, f32[128,128]{0,1:T(8,128)S(1)}, f32[255,128]{0,1:T(8,128)S(1)}, s32[]{:T(128)}, /*index=5*/s32[]{:T(128)}) %tuple.94), condition=%wide.region_3.0_spmd.clone, body=%wide.region_2.0_spmd.clone.sunk | while | flops 49155 | bytes 460375 | solution.py:36
  459.7 10.5 %convolution_bitcast_fusion = f32[8192,128]{1,0:T(8,128)} fusion(f32[8192,3,128]{0,2,1:T(8,128)} %mul.89, bf16[8192,3,128]{0,2,1:T(8,128)(2,1)} %all-gather.4.cloned.1.call-done, bf16[128,1,128]{0,2,1:T(8,128)(2,1)S(1)} %get-tuple-element.260, bf16[128,1,128]{0,2,1:T(8,128)(2,1)S(1)} %get-tuple-element.259, bf16[128,1,128]{0,2,1:T(8,128)(2,1)S(1)} %fusion.9), kind=kOutput, calls=%fused_computation.9 | convolution fusion | flops 814841856 | bytes 23166976 | tf_op jit(solution)/shard_map/dot_general | solution.py:102
  470.2 1.0 fusion.13
  471.2 0.6 reshape.58
  471.9 0.1 slice_reduce_fusion
  472.1 16.3 %psum.7 = f32[8,128]{1,0:T(8,128)} all-reduce(f32[8,128]{1,0:T(8,128)S(1)} %broadcast_multiply_fusion), channel_id=1, replica_groups=mesh['fsdp'=8,'tensor'=64] {'fsdp'}, use_global_device_ids=true, to_apply=%region_6.0 | all-reduce | flops 1024 | bytes 8192 | tf_op jit(solution)/shard_map/psum | solution.py:111
  488.5 204.9 %reduce-scatter.2.cloned.1.call-done = f32[128,128]{1,0:T(8,128)} async-done(((f32[8192,128]{1,0:T(8,128)}), f32[128,128]{1,0:T(8,128)}) %reduce-scatter.2.cloned.1.call-update) | async-done | bytes 65552 | tf_op jit(solution)/shard_map/reduce_scatter | solution.py:101
  693.4 0.8 convert_bitcast_fusion
  694.2 0.7 copy.28
  (1034 shorter events, 52.1 us)
Async XLA Ops:
  7.2 25.2 %copy-start = (bf16[8,3,128]{2,0,1:T(8,128)(2,1)S(1)}, bf16[8,3,128]{2,0,1:T(8,128)(2,1)}, u32[]{:S(2)}) copy-start(bf16[8,3,128]{2,0,1:T(8,128)(2,1)} %param.12) | copy-start | bytes 18436
  7.2 167.3 %all-gather.4.cloned.1.call-start = ((), (), s32[]{:S(2)}) async-start(), calls=%async_computation.2 | async-start | bytes 7077888 | tf_op jit(solution)/shard_map/all_gather | solution.py:66
  12.2 358.0 %all-to-all-start = ((bf16[64,128,128]{1,2,0:T(8,128)(2,1)}), bf16[64,128,128]{1,2,0:T(8,128)(2,1)S(1)}, u32[]{:S(2)}, u32[]{:S(2)}) async-start(bf16[64,128,128]{1,2,0:T(8,128)(2,1)} %stack.14), calls=%async_computation | async-start | bytes 4194304 | tf_op jit(solution)/shard_map/all_to_all | solution.py:87
  30.8 285.2 %all-gather.8.cloned.1.call-start = ((), (), s32[]{:S(2)}) async-start(), calls=%async_computation.4 | async-start | bytes 2129920 | tf_op jit(solution)/shard_map/all_gather | solution.py:64
  31.6 338.7 %all-gather.6.cloned.1.call-start = ((), (), s32[]{:S(2)}) async-start(), calls=%async_computation.3 | async-start | bytes 2359296 | tf_op jit(solution)/shard_map/all_gather | solution.py:56
  32.3 661.1 %reduce-scatter.2.cloned.1.call-start = ((), (), s32[]{:S(2)}) async-start(), calls=%async_computation.5 | async-start | bytes 4259840 | tf_op jit(solution)/shard_map/reduce_scatter | solution.py:101
  372.6 20.9 %collective-permute-start = (bf16[127,128]{0,1:T(8,128)(2,1)S(1)}, bf16[127,128]{0,1:T(8,128)(2,1)S(1)}, u32[]{:S(2)}, u32[]{:S(2)}) collective-permute-start(bf16[127,128]{0,1:T(8,128)(2,1)S(1)} %slice.49), channel_id=1, source_target_pairs={{0,64},{64,128},{128,192},{192,256},{256,320},{320,384},{384,448},... | collective-permute-start | bytes 97544 | tf_op jit(solution)/shard_map/ppermute | solution.py:12
  376.0 13.8 %copy-start.1 = (f32[8,128]{1,0:T(8,128)S(1)}, f32[8,128]{1,0:T(8,128)}, u32[]{:S(2)}) copy-start(f32[8,128]{1,0:T(8,128)} %param.13) | copy-start | bytes 12292
  390.0 37.0 %collective-permute-start.1 = (bf16[127,128]{0,1:T(8,128)(2,1)S(1)}, bf16[127,128]{0,1:T(8,128)(2,1)S(1)}, u32[]{:S(2)}, u32[]{:S(2)}) collective-permute-start(bf16[127,128]{0,1:T(8,128)(2,1)S(1)} %slice.48), channel_id=1, source_target_pairs={{64,0},{128,64},{192,128},{256,192},{320,256},{384,320},{448,384},... | collective-permute-start | bytes 97544 | tf_op jit(solution)/shard_map/ppermute | solution.py:12
Sparse Core Ops, SparseCore 0:
  10.1 164.2 all-gather.3
  177.4 138.5 all-gather.7
  318.1 52.1 all-gather.5
  470.3 223.0 reduce-scatter.1
